TPU v7x, 256 devices: a whole 4x4x8 slice. The times are simulated.
256 devices in a mesh: lat: 16 (over z, core), lon: 16 (over y, x).
Axes of the slice: x: 4, y: 4, z: 8, core: 2. Of those that a mesh axis runs over, the one named last changes fastest.
Arguments:
- density: float32 [75, 256, 4096], P(None, 'lat', 'lon'), may hold values from -24 to 24
- tend_east: float32 [75, 256, 4096], P(None, 'lat', 'lon'), may hold values from -6 to 6
- tend_north: float32 [75, 256, 4096], P(None, 'lat', 'lon'), may hold values from -6 to 6
- thickness: float32 [75], replicated, may hold values from 0.02 to 0.2
- levels: int32 [256, 4096], P('lat', 'lon'), may hold values from 1 to 75
- ocean_mask: int32 [256, 4096], P('lat', 'lon'), may hold values 0 or 1
- eta_prev: float32 [256, 4096], P('lat', 'lon'), may hold values from -1.2 to 1.2
- coarse: float32 [4096, 4096], P(('lat', 'lon')), as said below
Outputs:
- surface: float32 [256, 4096], P('lat', 'lon')
- precond_residual: float32 [256, 4096], P('lat', 'lon')
Inputs may be any that keep to these rules, and one draw needn't show every extreme that they name: coarse is symmetric positive definite.
All inputs are finite; a program needn't handle non-finite values. No bound on the sum of `ocean_mask` on one device may be relied on, other than what follows from the above.
Results may differ from a plain program's by a relative error of at most 0.0003.
Values sent between devices are 32-bit elements; how exact they have to be, the bound alone decides.
No kernel may reach another device: no remote copies, remote signals or barrier semaphores. Data moves between devices by JAX's collectives and lax.ppermute only.
A program may use at most 64 MiB of HBM per device.

v0:
```python
import jax
import jax.numpy as jnp
from jax import lax
from jax.sharding import PartitionSpec as P

K = 75
TILE_SIDE = 4
ITERS = 2
surface_coeff = 0.25
highest = lax.Precision.HIGHEST


def with_halo(shard, sides, width):
    for axis, dim in sides:
        peers, length = (lax.axis_size(axis), shard.shape[dim])
        up = [(i, (i + 1) % peers) for i in range(peers)]
        down = [(j, i) for i, j in up]
        last = lax.slice_in_dim(shard, length - width, length, axis=dim)
        leading = lax.slice_in_dim(shard, 0, width, axis=dim)
        before = lax.ppermute(last, axis, up)
        after = lax.ppermute(leading, axis, down)
        shard = jnp.concatenate([before, shard, after], axis=dim)
    return shard


def wall_rows(framed, rim_width):
    row_count = framed.shape[1]
    row_index = lax.broadcasted_iota(jnp.int32, (1, row_count, 1), 1)
    position = lax.axis_index("lat")
    last_index = lax.axis_size("lat") - 1
    southern = jnp.logical_and(position == 0, row_index < rim_width)
    northern = jnp.logical_and(position == last_index, row_index >= row_count - rim_width)
    return jnp.where(jnp.logical_or(southern, northern), 0.0, framed)


def plane_halo(planes):
    return wall_rows(with_halo(planes, (("lat", 1), ("lon", 2)), 1), 1)


def global_sum(partial_value):
    return lax.psum(partial_value, ("lat", "lon"))


def gather_coarse(own_values):
    return lax.all_gather(own_values, ("lat", "lon"), axis=0, tiled=True)


def restrict_local(values, ocean_share):
    tile_rows = values.shape[0] // TILE_SIDE
    tile_cols = values.shape[1] // TILE_SIDE
    tiled_sum = (values * ocean_share).reshape(TILE_SIDE, tile_rows, TILE_SIDE, tile_cols)
    return jnp.sum(tiled_sum, axis=(1, 3)).reshape(-1)


def prolong_local(coarse_values, ocean_share):
    tile_rows = ocean_share.shape[0] // TILE_SIDE
    tile_cols = ocean_share.shape[1] // TILE_SIDE
    blocks = coarse_values.reshape(TILE_SIDE, 1, TILE_SIDE, 1)
    spread = jnp.broadcast_to(blocks, (TILE_SIDE, tile_rows, TILE_SIDE, tile_cols))
    return spread.reshape(ocean_share.shape) * ocean_share


def east_fourth(own_rows):
    return (
        8.0 * (own_rows[:, :, 3:-1] - own_rows[:, :, 1:-3])
        - (own_rows[:, :, 4:] - own_rows[:, :, :-4])
    ) / 12.0


def north_fourth(own_cols):
    return (
        8.0 * (own_cols[:, 3:-1, :] - own_cols[:, 1:-3, :])
        - (own_cols[:, 4:, :] - own_cols[:, :-4, :])
    ) / 12.0


def apply_operator(face_list, diagonal, values, beside_all):
    east_face, west_face, north_face, south_face = face_list
    return diagonal * values - (
        east_face * beside_all[1:-1, 2:]
        + west_face * beside_all[1:-1, :-2]
        + north_face * beside_all[2:, 1:-1]
        + south_face * beside_all[:-2, 1:-1]
    )


def body(density, tend_east, tend_north, thickness, levels, ocean_mask, eta_prev, coarse):
    wet_levels = levels * ocean_mask
    ocean_share = ocean_mask.astype(jnp.float32)
    layer_weight = thickness[:, None, None]
    depth_index = lax.broadcasted_iota(jnp.int32, (K,) + wet_levels.shape, 0)
    active = (depth_index < wet_levels[None]).astype(jnp.float32)
    lower_ones = (
        lax.broadcasted_iota(jnp.int32, (K, K), 1) <= lax.broadcasted_iota(jnp.int32, (K, K), 0)
    ).astype(jnp.float32)
    pressure = (
        jnp.einsum("kj,jab->kab", lower_ones, layer_weight * density, precision=highest) * active
    )
    solution = ocean_share * eta_prev
    framed = wall_rows(with_halo(pressure, (("lat", 1), ("lon", 2)), 2), 2)
    east_diff = east_fourth(framed[:, 2:-2, :])
    north_diff = north_fourth(framed[:, :, 2:-2])
    force_east = jnp.sum(layer_weight * active * (tend_east - east_diff), axis=0)
    force_north = jnp.sum(layer_weight * active * (tend_north - north_diff), axis=0)
    column_depth = jnp.sum(layer_weight * active, axis=0)
    planes = plane_halo(jnp.stack([force_east, force_north, column_depth, solution]))
    right_side = (
        ocean_share
        * 0.5
        * (planes[0, 1:-1, :-2] - planes[0, 1:-1, 2:] + planes[1, :-2, 1:-1] - planes[1, 2:, 1:-1])
    )
    depth_framed = planes[2]
    solution_framed = planes[3]
    center = depth_framed[1:-1, 1:-1]
    face_list = (
        jnp.minimum(center, depth_framed[1:-1, 2:]),
        jnp.minimum(center, depth_framed[1:-1, :-2]),
        jnp.minimum(center, depth_framed[2:, 1:-1]),
        jnp.minimum(center, depth_framed[:-2, 1:-1]),
    )
    diagonal = ocean_share * (
        surface_coeff + face_list[0] + face_list[1] + face_list[2] + face_list[3]
    ) + (1.0 - ocean_share)

    def precondition(values):
        coarse_all = gather_coarse(restrict_local(values, ocean_share))
        return values / diagonal + prolong_local(
            jnp.dot(coarse, coarse_all, precision=highest), ocean_share
        )

    residual = right_side - apply_operator(face_list, diagonal, solution, solution_framed)
    precond = precondition(residual)
    direction = precond
    rz_now = global_sum(jnp.sum(residual * precond))
    for iteration in range(ITERS):
        beside_all = plane_halo(direction[None])[0]
        image_field = apply_operator(face_list, diagonal, direction, beside_all)
        step_length = rz_now / global_sum(jnp.sum(direction * image_field))
        solution = solution + step_length * direction
        residual = residual - step_length * image_field
        precond = precondition(residual)
        if iteration + 1 < ITERS:
            rz_next = global_sum(jnp.sum(residual * precond))
            direction = precond + rz_next / rz_now * direction
            rz_now = rz_next
    return (solution, precond)


def solution(mesh):
    return jax.shard_map(
        body,
        mesh=mesh,
        in_specs=(
            P(None, "lat", "lon"),
            P(None, "lat", "lon"),
            P(None, "lat", "lon"),
            P(),
            P("lat", "lon"),
            P("lat", "lon"),
            P("lat", "lon"),
            P(("lat", "lon"), None),
        ),
        out_specs=(P("lat", "lon"), P("lat", "lon")),
        check_vma=False,
    )
```

profile of v0, /device:TPU:1, one launch (start us, length us, event | category | flops | bytes accessed | tf_op | source)
XLA Modules:
  0.0 525.2 jit_solution(2610545018374523092)
XLA Ops:
  0.6 0.8 mul.159
  1.4 0.6 copy-done.5
  2.0 2.8 convolution_select_fusion
  4.9 3.0 collective-permute-start
  8.2 0.6 fusion.28
  8.8 1.4 collective-permute-done
  10.2 2.8 collective-permute-done.1
  13.1 0.3 fusion.34
  13.4 0.9 copy.25
  14.3 1.2 collective-permute-start.2
  15.5 0.3 copy.26
  15.8 3.8 collective-permute-start.3
  19.6 0.5 and_or_fusion
  20.2 0.5 collective-permute-done.2
  20.6 0.4 copy.27
  21.0 1.1 copy.28
  22.2 1.7 maximum_select_fusion
  23.9 2.6 fusion
  26.6 0.7 collective-permute-start.4
  27.3 2.1 collective-permute-start.5
  29.4 0.6 collective-permute-done.4
  30.0 0.3 collective-permute-done.5
  30.5 5.0 collective-permute-start.7
  35.5 1.4 collective-permute-done.6
  37.6 82.0 %all-reduce = f32[4096]{0:T(1024)S(1)} all-reduce(f32[4096]{0:T(1024)S(1)} %dynamic-update-slice), channel_id=1, replica_groups=mesh['lat'=16,'lon'=16] {'lat','lon'}, use_global_device_ids=true, to_apply=%add | all-reduce | flops 4096 | bytes 32768
  119.7 0.4 convolution_bitcast_fusion.2
  120.4 1.0 collective-permute-start.9
  121.4 0.6 collective-permute-done.8
  122.0 1.4 collective-permute-done.9
  123.5 4.8 collective-permute-start.11
  128.3 1.1 collective-permute-done.10
  129.5 0.7 multiply_reduce_fusion.2
  130.2 79.6 %all-reduce.3 = (f32[]{:T(128)}, f32[]{:T(128)}) all-reduce(f32[]{:T(128)} %get-tuple-element.6, f32[]{:T(128)} %get-tuple-element.5), channel_id=1, replica_groups=mesh['lat'=16,'lon'=16] {'lat','lon'}, use_global_device_ids=true, to_apply=%region_5.6 | all-reduce | flops 2 | bytes 16 | tf_op jit(solution)/shard_map/psum | solution.py:41
  211.6 72.8 %all-reduce.1 = f32[4096]{0:T(1024)S(1)} all-reduce(f32[4096]{0:T(1024)S(1)} %dynamic-update-slice.1), channel_id=1, replica_groups=mesh['lat'=16,'lon'=16] {'lat','lon'}, use_global_device_ids=true, to_apply=%add.1 | all-reduce | flops 4096 | bytes 32768
  284.4 0.4 convolution_bitcast_fusion.1
  285.1 0.6 multiply_reduce_fusion.1
  285.7 73.5 %psum.30 = f32[]{:T(128)} all-reduce(f32[]{:T(128)} %multiply_reduce_fusion.1), channel_id=1, replica_groups=mesh['lat'=16,'lon'=16] {'lat','lon'}, use_global_device_ids=true, to_apply=%region_10.11 | all-reduce | flops 1 | bytes 8 | tf_op jit(solution)/shard_map/psum | solution.py:41
  360.5 1.5 collective-permute-start.12
  362.0 0.7 collective-permute-done.12
  362.8 2.3 collective-permute-done.13
  365.1 0.7 collective-permute-start.14
  365.8 4.1 collective-permute-start.15
  369.9 1.1 collective-permute-done.14
  371.1 0.7 multiply_reduce_fusion
  371.8 77.7 %psum.31 = f32[]{:T(128)} all-reduce(f32[]{:T(128)} %get-tuple-element.9), channel_id=1, replica_groups=mesh['lat'=16,'lon'=16] {'lat','lon'}, use_global_device_ids=true, to_apply=%region_12.13 | all-reduce | flops 1 | bytes 8 | tf_op jit(solution)/shard_map/psum | solution.py:41
  451.3 72.6 %all-reduce.2 = f32[4096]{0:T(1024)S(1)} all-reduce(f32[4096]{0:T(1024)S(1)} %dynamic-update-slice.2), channel_id=1, replica_groups=mesh['lat'=16,'lon'=16] {'lat','lon'}, use_global_device_ids=true, to_apply=%add.2 | all-reduce | flops 4096 | bytes 32768
  523.9 0.4 convolution_bitcast_fusion
  524.5 0.6 multiply_add_fusion
  (73 shorter events, 3.5 us)
Async XLA Ops:
  0.6 119.0 %copy-start = (f32[16,4096]{1,0:T(8,128)S(1)}, f32[16,4096]{1,0:T(8,128)}, u32[]{:S(2)}) copy-start(f32[16,4096]{1,0:T(8,128)} %param.15) | copy-start | bytes 786436
  1.4 0.6 copy-start.5
  2.0 6.1 %copy-start.1 = (s32[16,256]{1,0:T(8,128)S(1)}, s32[16,256]{1,0:T(8,128)}, u32[]{:S(2)}) copy-start(s32[16,256]{1,0:T(8,128)} %param.13) | copy-start | bytes 49156
  2.0 6.1 %copy-start.7 = (f32[16,256]{1,0:T(8,128)S(1)}, f32[16,256]{1,0:T(8,128)}, u32[]{:S(2)}) copy-start(f32[16,256]{1,0:T(8,128)} %param.14) | copy-start | bytes 49156
  4.9 5.3 %collective-permute-start = (f32[75,2,256]{2,0,1:T(8,128)S(1)}, f32[75,2,256]{2,0,1:T(8,128)S(1)}, u32[]{:S(2)}, u32[]{:S(2)}) collective-permute-start(f32[75,2,256]{2,0,1:T(8,128)S(1)} %get-tuple-element.23), channel_id=1, source_target_pairs={{0,16},{16,32},{32,48},{48,64},{64,80},{80,96},{96,112},{112,128},... | collective-permute-start | bytes 460808 | tf_op jit(solution)/shard_map/ppermute | solution.py:20
  7.9 5.0 collective-permute-start.1
  14.3 6.3 %collective-permute-start.2 = (f32[75,20,2]{0,2,1:T(2,128)}, f32[75,20,2]{0,2,1:T(2,128)S(1)}, u32[]{:S(2)}, u32[]{:S(2)}) collective-permute-start(f32[75,20,2]{0,2,1:T(2,128)} %copy.25), channel_id=1, source_target_pairs={{0,1},{1,2},{2,3},{3,4},{4,5},{5,6},{6,7},{7,8},{8,9},{9,10},{10,1... | collective-permute-start | bytes 36008 | tf_op jit(solution)/shard_map/ppermute | solution.py:20
  15.8 5.2 collective-permute-start.3
  22.1 1.8 copy-start.2
  22.1 1.8 copy-start.3
  22.1 1.8 copy-start.6
  22.1 1.8 copy-start.9
  23.9 2.6 copy-start.4
  23.9 13.1 %copy-start.8 = (f32[16,256]{1,0:T(8,128)S(1)}, f32[16,256]{1,0:T(8,128)}, u32[]{:S(2)}) copy-start(f32[16,256]{1,0:T(8,128)} %param.14) | copy-start | bytes 49156
  26.6 3.4 collective-permute-start.4
  27.3 3.0 collective-permute-start.5
  30.4 6.4 %collective-permute-start.6 = (f32[4,18,1]{2,1,0:T(8,128)S(1)}, f32[4,18,1]{2,1,0:T(8,128)S(1)}, u32[]{:S(2)}, u32[]{:S(2)}) collective-permute-start(f32[4,18,1]{2,1,0:T(8,128)S(1)} %get-tuple-element.27), channel_id=1, source_target_pairs={{0,1},{1,2},{2,3},{3,4},{4,5},{5,6},{6,7},{7,8},{8,9},{9,10},{10,1... | collective-permute-start | bytes 872 | tf_op jit(solution)/shard_map/ppermute | solution.py:20
  30.5 6.4 %collective-permute-start.7 = (f32[4,18,1]{2,1,0:T(8,128)S(1)}, f32[4,18,1]{2,1,0:T(8,128)S(1)}, u32[]{:S(2)}, u32[]{:S(2)}) collective-permute-start(f32[4,18,1]{2,1,0:T(8,128)S(1)} %get-tuple-element.28), channel_id=1, source_target_pairs={{1,0},{2,1},{3,2},{4,3},{5,4},{6,5},{7,6},{8,7},{9,8},{10,9},{11,1... | collective-permute-start | bytes 872 | tf_op jit(solution)/shard_map/ppermute | solution.py:21
  120.4 1.7 collective-permute-start.8
  120.4 3.0 collective-permute-start.9
  123.5 5.9 %collective-permute-start.10 = (f32[1,18,1]{2,1,0:T(8,128)S(1)}, f32[1,18,1]{2,1,0:T(8,128)S(1)}, u32[]{:S(2)}, u32[]{:S(2)}) collective-permute-start(f32[1,18,1]{2,1,0:T(8,128)S(1)} %get-tuple-element.33), channel_id=1, source_target_pairs={{0,1},{1,2},{2,3},{3,4},{4,5},{5,6},{6,7},{7,8},{8,9},{9,10},{10,1... | collective-permute-start | bytes 224 | tf_op jit(solution)/shard_map/ppermute | solution.py:20
  123.5 5.9 %collective-permute-start.11 = (f32[1,18,1]{2,1,0:T(8,128)S(1)}, f32[1,18,1]{2,1,0:T(8,128)S(1)}, u32[]{:S(2)}, u32[]{:S(2)}) collective-permute-start(f32[1,18,1]{2,1,0:T(8,128)S(1)} %get-tuple-element.34), channel_id=1, source_target_pairs={{1,0},{2,1},{3,2},{4,3},{5,4},{6,5},{7,6},{8,7},{9,8},{10,9},{11,1... | collective-permute-start | bytes 224 | tf_op jit(solution)/shard_map/ppermute | solution.py:21
  360.5 2.3 collective-permute-start.12
  362.0 3.0 collective-permute-start.13
  365.1 5.9 %collective-permute-start.14 = (f32[1,18,1]{2,1,0:T(8,128)S(1)}, f32[1,18,1]{2,1,0:T(8,128)S(1)}, u32[]{:S(2)}, u32[]{:S(2)}) collective-permute-start(f32[1,18,1]{2,1,0:T(8,128)S(1)} %get-tuple-element.31), channel_id=1, source_target_pairs={{0,1},{1,2},{2,3},{3,4},{4,5},{5,6},{6,7},{7,8},{8,9},{9,10},{10,1... | collective-permute-start | bytes 224 | tf_op jit(solution)/shard_map/ppermute | solution.py:20
  365.8 5.2 collective-permute-start.15
where the time goes:
time: 527 us; the launch traced here: 525 us
  blocking collectives  458 us (87%)
  starting transfers between devices  28.2 us (5%)
  waiting for transfers between devices  14.2 us (3%)
  other arithmetic  9.79 us (2%)
  local copies, waits for them, and re-layouts  5.91 us (1%)
    psum x3, blocking collectives, global_sum(): return lax.psum(partial_value, ('lat', 'lon'))  231 us
    unnamed x3, blocking collectives  227 us
    ppermute x8, starting transfers between devices, with_halo(): after = lax.ppermute(leading, axis, down)  20.9 us
  transfers between devices with their start and end apart: 16, of which 12 were waited for; matrix products, arithmetic and copies ran while one was open for 0% of the time, Pallas kernels for 0%

commit v1 on v0

--- a/solution.py
+++ b/solution.py
@@ -2,6 +2,7 @@
 import jax.numpy as jnp
 from jax import lax
 from jax.sharding import PartitionSpec as P
+from jax.lax import psum
 
 K = 75
 TILE_SIDE = 4
@@ -38,7 +39,12 @@
 
 
 def global_sum(partial_value):
-    return lax.psum(partial_value, ("lat", "lon"))
+
+    def unit_refer(base_x):
+        inter = psum(psum(base_x, "lon"), "lat")
+        return inter
+
+    return unit_refer(partial_value)
 
 
 def gather_coarse(own_values):

time: 527 us -> 492 us (0.934)
  blocking collectives: 458 us -> 426 us
    psum x3 -> x6, blocking collectives: 231 us -> 198 us  [unit_refer(): inter = psum(psum(base_x, 'lon'), 'lat')]
where the time goes in v1:
time: 492 us; the launch traced here: 491 us
  blocking collectives  426 us (87%)
  starting transfers between devices  27.4 us (6%)
  waiting for transfers between devices  13.5 us (3%)
  other arithmetic  9.79 us (2%)
  local copies, waits for them, and re-layouts  5.91 us (1%)
  between operations  4.96 us (1%)
    unnamed x3, blocking collectives  228 us
    psum x6, blocking collectives, unit_refer(): inter = psum(psum(base_x, 'lon'), 'lat')  198 us
    ppermute x8, starting transfers between devices, with_halo(): after = lax.ppermute(leading, axis, down)  21.8 us
  transfers between devices with their start and end apart: 16, of which 12 were waited for; matrix products, arithmetic and copies ran while one was open for 0% of the time, Pallas kernels for 0%

profile of v1, /device:TPU:1, one launch (start us, length us, event | category | flops | bytes accessed | tf_op | source)
XLA Modules:
  0.0 491.2 jit_solution(8075738755638618896)
XLA Ops:
  0.6 0.8 mul.159
  1.4 0.6 copy-done.5
  2.0 2.8 convolution_select_fusion
  4.9 3.0 collective-permute-start
  8.2 0.6 fusion.28
  8.8 1.4 collective-permute-done
  10.2 2.8 collective-permute-done.1
  13.4 0.9 copy.25
  14.3 1.2 collective-permute-start.2
  15.8 3.8 collective-permute-start.3
  19.6 0.5 and_or_fusion
  20.2 0.5 collective-permute-done.2
  20.6 0.4 copy.27
  21.0 1.1 copy.28
  22.2 1.7 maximum_select_fusion
  23.9 2.6 fusion
  26.6 0.7 collective-permute-start.4
  27.3 2.1 collective-permute-start.5
  29.4 0.6 collective-permute-done.4
  30.5 5.0 %collective-permute-start.7 = (f32[4,18,1]{2,1,0:T(8,128)S(1)}, f32[4,18,1]{2,1,0:T(8,128)S(1)}, u32[]{:S(2)}, u32[]{:S(2)}) collective-permute-start(f32[4,18,1]{2,1,0:T(8,128)S(1)} %get-tuple-element.30), channel_id=1, source_target_pairs={{1,0},{2,1},{3,2},{4,3},{5,4},{6,5},{7,6},{8,7},{9,8},{10,9},{11,1... | collective-permute-start | bytes 872 | tf_op jit(solution)/shard_map/ppermute | solution.py:22
  35.5 1.4 collective-permute-done.6
  37.6 82.0 %all-reduce = f32[4096]{0:T(1024)S(1)} all-reduce(f32[4096]{0:T(1024)S(1)} %dynamic-update-slice), channel_id=1, replica_groups=mesh['lat'=16,'lon'=16] {'lat','lon'}, use_global_device_ids=true, to_apply=%add | all-reduce | flops 4096 | bytes 32768
  119.7 0.4 convolution_bitcast_fusion.2
  120.4 1.0 collective-permute-start.9
  121.4 0.6 collective-permute-done.8
  122.0 1.4 collective-permute-done.9
  123.5 4.8 collective-permute-start.11
  128.3 1.1 collective-permute-done.10
  129.5 0.7 multiply_reduce_fusion.2
  130.2 34.2 %all-reduce.3 = (f32[]{:T(128)}, f32[]{:T(128)}) all-reduce(f32[]{:T(128)} %get-tuple-element.6, f32[]{:T(128)} %get-tuple-element.5), channel_id=1, replica_groups=mesh['lat'=16,'lon'=16] {'lon'}, use_global_device_ids=true, to_apply=%region_5.6 | all-reduce | flops 2 | bytes 16 | tf_op jit(solution)/shard_map/psum | solution.py:44
  164.3 34.2 %all-reduce.4 = (f32[]{:T(128)}, f32[]{:T(128)}) all-reduce(f32[]{:T(128)} %get-tuple-element.7, f32[]{:T(128)} %get-tuple-element.8), channel_id=1, replica_groups=mesh['lat'=16,'lon'=16] {'lat'}, use_global_device_ids=true, to_apply=%region_6.7 | all-reduce | flops 2 | bytes 16 | tf_op jit(solution)/shard_map/psum | solution.py:44
  200.3 72.8 %all-reduce.1 = f32[4096]{0:T(1024)S(1)} all-reduce(f32[4096]{0:T(1024)S(1)} %dynamic-update-slice.1), channel_id=1, replica_groups=mesh['lat'=16,'lon'=16] {'lat','lon'}, use_global_device_ids=true, to_apply=%add.1 | all-reduce | flops 4096 | bytes 32768
  273.1 0.4 convolution_bitcast_fusion.1
  273.8 0.6 multiply_reduce_fusion.1
  274.4 30.3 %psum.60 = f32[]{:T(128)} all-reduce(f32[]{:T(128)} %multiply_reduce_fusion.1), channel_id=1, replica_groups=mesh['lat'=16,'lon'=16] {'lon'}, use_global_device_ids=true, to_apply=%region_12.13 | all-reduce | flops 1 | bytes 8 | tf_op jit(solution)/shard_map/psum | solution.py:44
  304.7 31.5 %psum.61 = f32[]{:T(128)} all-reduce(f32[]{:T(128)} %psum.60), channel_id=1, replica_groups=mesh['lat'=16,'lon'=16] {'lat'}, use_global_device_ids=true, to_apply=%region_13.14 | all-reduce | flops 1 | bytes 8 | tf_op jit(solution)/shard_map/psum | solution.py:44
  337.5 0.7 collective-permute-start.13
  338.2 0.6 collective-permute-done.12
  338.8 1.7 collective-permute-done.13
  340.6 0.5 collective-permute-start.14
  341.2 4.3 collective-permute-start.15
  345.4 1.1 collective-permute-done.14
  346.6 0.7 multiply_reduce_fusion
  347.3 33.9 %psum.62 = f32[]{:T(128)} all-reduce(f32[]{:T(128)} %get-tuple-element.11), channel_id=1, replica_groups=mesh['lat'=16,'lon'=16] {'lon'}, use_global_device_ids=true, to_apply=%region_15.16 | all-reduce | flops 1 | bytes 8 | tf_op jit(solution)/shard_map/psum | solution.py:44
  381.2 34.0 %psum.63 = f32[]{:T(128)} all-reduce(f32[]{:T(128)} %psum.62), channel_id=1, replica_groups=mesh['lat'=16,'lon'=16] {'lat'}, use_global_device_ids=true, to_apply=%region_16.17 | all-reduce | flops 1 | bytes 8 | tf_op jit(solution)/shard_map/psum | solution.py:44
  417.1 72.8 %all-reduce.2 = f32[4096]{0:T(1024)S(1)} all-reduce(f32[4096]{0:T(1024)S(1)} %dynamic-update-slice.2), channel_id=1, replica_groups=mesh['lat'=16,'lon'=16] {'lat','lon'}, use_global_device_ids=true, to_apply=%add.2 | all-reduce | flops 4096 | bytes 32768
  489.9 0.4 convolution_bitcast_fusion
  490.5 0.6 multiply_add_fusion
  (76 shorter events, 4.5 us)
Async XLA Ops:
  0.6 119.0 %copy-start = (f32[16,4096]{1,0:T(8,128)S(1)}, f32[16,4096]{1,0:T(8,128)}, u32[]{:S(2)}) copy-start(f32[16,4096]{1,0:T(8,128)} %param.15) | copy-start | bytes 786436
  1.4 0.6 copy-start.5
  2.0 6.1 %copy-start.1 = (s32[16,256]{1,0:T(8,128)S(1)}, s32[16,256]{1,0:T(8,128)}, u32[]{:S(2)}) copy-start(s32[16,256]{1,0:T(8,128)} %param.13) | copy-start | bytes 49156
  2.0 6.1 %copy-start.7 = (f32[16,256]{1,0:T(8,128)S(1)}, f32[16,256]{1,0:T(8,128)}, u32[]{:S(2)}) copy-start(f32[16,256]{1,0:T(8,128)} %param.14) | copy-start | bytes 49156
  4.9 5.3 %collective-permute-start = (f32[75,2,256]{2,0,1:T(8,128)S(1)}, f32[75,2,256]{2,0,1:T(8,128)S(1)}, u32[]{:S(2)}, u32[]{:S(2)}) collective-permute-start(f32[75,2,256]{2,0,1:T(8,128)S(1)} %get-tuple-element.25), channel_id=1, source_target_pairs={{0,16},{16,32},{32,48},{48,64},{64,80},{80,96},{96,112},{112,128},... | collective-permute-start | bytes 460808 | tf_op jit(solution)/shard_map/ppermute | solution.py:21
  7.9 5.0 %collective-permute-start.1 = (f32[75,2,256]{2,0,1:T(8,128)S(1)}, f32[75,2,256]{2,0,1:T(8,128)S(1)}, u32[]{:S(2)}, u32[]{:S(2)}) collective-permute-start(f32[75,2,256]{2,0,1:T(8,128)S(1)} %get-tuple-element.26), channel_id=1, source_target_pairs={{16,0},{32,16},{48,32},{64,48},{80,64},{96,80},{112,96},{128,112},... | collective-permute-start | bytes 460808 | tf_op jit(solution)/shard_map/ppermute | solution.py:22
  14.3 6.3 %collective-permute-start.2 = (f32[75,20,2]{0,2,1:T(2,128)}, f32[75,20,2]{0,2,1:T(2,128)S(1)}, u32[]{:S(2)}, u32[]{:S(2)}) collective-permute-start(f32[75,20,2]{0,2,1:T(2,128)} %copy.25), channel_id=1, source_target_pairs={{0,1},{1,2},{2,3},{3,4},{4,5},{5,6},{6,7},{7,8},{8,9},{9,10},{10,1... | collective-permute-start | bytes 36008 | tf_op jit(solution)/shard_map/ppermute | solution.py:21
  15.8 5.2 %collective-permute-start.3 = (f32[75,20,2]{0,2,1:T(2,128)S(1)}, f32[75,20,2]{0,2,1:T(2,128)}, u32[]{:S(2)}, u32[]{:S(2)}) collective-permute-start(f32[75,20,2]{0,2,1:T(2,128)S(1)} %copy.26), channel_id=1, source_target_pairs={{1,0},{2,1},{3,2},{4,3},{5,4},{6,5},{7,6},{8,7},{9,8},{10,9},{11,1... | collective-permute-start | bytes 36008 | tf_op jit(solution)/shard_map/ppermute | solution.py:22
  22.1 1.8 copy-start.2
  22.1 1.8 copy-start.3
  22.1 1.8 copy-start.6
  22.1 1.8 copy-start.9
  23.9 2.6 copy-start.4
  23.9 13.1 %copy-start.8 = (f32[16,256]{1,0:T(8,128)S(1)}, f32[16,256]{1,0:T(8,128)}, u32[]{:S(2)}) copy-start(f32[16,256]{1,0:T(8,128)} %param.14) | copy-start | bytes 49156
  26.6 3.4 collective-permute-start.4
  27.3 3.0 collective-permute-start.5
  30.4 6.4 %collective-permute-start.6 = (f32[4,18,1]{2,1,0:T(8,128)S(1)}, f32[4,18,1]{2,1,0:T(8,128)S(1)}, u32[]{:S(2)}, u32[]{:S(2)}) collective-permute-start(f32[4,18,1]{2,1,0:T(8,128)S(1)} %get-tuple-element.29), channel_id=1, source_target_pairs={{0,1},{1,2},{2,3},{3,4},{4,5},{5,6},{6,7},{7,8},{8,9},{9,10},{10,1... | collective-permute-start | bytes 872 | tf_op jit(solution)/shard_map/ppermute | solution.py:21
  30.5 6.4 %collective-permute-start.7 = (f32[4,18,1]{2,1,0:T(8,128)S(1)}, f32[4,18,1]{2,1,0:T(8,128)S(1)}, u32[]{:S(2)}, u32[]{:S(2)}) collective-permute-start(f32[4,18,1]{2,1,0:T(8,128)S(1)} %get-tuple-element.30), channel_id=1, source_target_pairs={{1,0},{2,1},{3,2},{4,3},{5,4},{6,5},{7,6},{8,7},{9,8},{10,9},{11,1... | collective-permute-start | bytes 872 | tf_op jit(solution)/shard_map/ppermute | solution.py:22
  120.4 1.7 collective-permute-start.8
  120.4 3.0 collective-permute-start.9
  123.5 5.9 %collective-permute-start.10 = (f32[1,18,1]{2,1,0:T(8,128)S(1)}, f32[1,18,1]{2,1,0:T(8,128)S(1)}, u32[]{:S(2)}, u32[]{:S(2)}) collective-permute-start(f32[1,18,1]{2,1,0:T(8,128)S(1)} %get-tuple-element.35), channel_id=1, source_target_pairs={{0,1},{1,2},{2,3},{3,4},{4,5},{5,6},{6,7},{7,8},{8,9},{9,10},{10,1... | collective-permute-start | bytes 224 | tf_op jit(solution)/shard_map/ppermute | solution.py:21
  123.5 5.9 %collective-permute-start.11 = (f32[1,18,1]{2,1,0:T(8,128)S(1)}, f32[1,18,1]{2,1,0:T(8,128)S(1)}, u32[]{:S(2)}, u32[]{:S(2)}) collective-permute-start(f32[1,18,1]{2,1,0:T(8,128)S(1)} %get-tuple-element.36), channel_id=1, source_target_pairs={{1,0},{2,1},{3,2},{4,3},{5,4},{6,5},{7,6},{8,7},{9,8},{10,9},{11,1... | collective-permute-start | bytes 224 | tf_op jit(solution)/shard_map/ppermute | solution.py:22
  337.5 1.3 collective-permute-start.12
  337.5 3.0 collective-permute-start.13
  340.6 5.9 %collective-permute-start.14 = (f32[1,18,1]{2,1,0:T(8,128)S(1)}, f32[1,18,1]{2,1,0:T(8,128)S(1)}, u32[]{:S(2)}, u32[]{:S(2)}) collective-permute-start(f32[1,18,1]{2,1,0:T(8,128)S(1)} %get-tuple-element.33), channel_id=1, source_target_pairs={{0,1},{1,2},{2,3},{3,4},{4,5},{5,6},{6,7},{7,8},{8,9},{9,10},{10,1... | collective-permute-start | bytes 224 | tf_op jit(solution)/shard_map/ppermute | solution.py:21
  341.2 5.3 %collective-permute-start.15 = (f32[1,18,1]{2,1,0:T(8,128)S(1)}, f32[1,18,1]{2,1,0:T(8,128)S(1)}, u32[]{:S(2)}, u32[]{:S(2)}) collective-permute-start(f32[1,18,1]{2,1,0:T(8,128)S(1)} %get-tuple-element.34), channel_id=1, source_target_pairs={{1,0},{2,1},{3,2},{4,3},{5,4},{6,5},{7,6},{8,7},{9,8},{10,9},{11,1... | collective-permute-start | bytes 224 | tf_op jit(solution)/shard_map/ppermute | solution.py:22
